TPU v7x, 32 devices: a whole 2x2x4 slice. The times are simulated.
32 devices in a mesh: rep: 4 (over x, core), shard: 8 (over z, y).
Axes of the slice: x: 2, y: 2, z: 4, core: 2. Of those that a mesh axis runs over, the one named last changes fastest.
Arguments:
- tokens: bfloat16 [4096, 2048], P(('rep', 'shard')), may hold values from -6 to 6
- segment_ids: int32 [4096], P(('rep', 'shard')), may hold values from 0 to 15, as said below
- positions: int32 [4096], P(('rep', 'shard')), may hold values from 0 to 127, as said below
- first_gain: float32 [2048], P('shard'), may hold values from 0.1 to 1.9
- first_shift: float32 [2048], P('shard'), may hold values from -1.75 to 1.75
- project_weight: bfloat16 [2048, 6144], P('shard'), may hold values from -0.125 to 0.125
- project_bias: float32 [6144], P('shard'), may hold values from -1.75 to 1.75
- mixing_weight: bfloat16 [2048, 2048], P('shard'), may hold values from -1 to 1
- mixing_bias: float32 [2048], P('shard'), may hold values from -1.75 to 1.75
- second_gain: float32 [2048], P('shard'), may hold values from 0.1 to 1.9
- second_shift: float32 [2048], P('shard'), may hold values from -1.75 to 1.75
- widen_weight: bfloat16 [2048, 8192], P('shard'), may hold values from -0.125 to 0.125
- widen_bias: float32 [8192], P('shard'), may hold values from -3 to 3
- narrow_weight: bfloat16 [8192, 2048], P('shard'), may hold values from -0.0625 to 0.0625
- narrow_bias: float32 [2048], P('shard'), may hold values from -1.75 to 1.75
- cotangent: bfloat16 [4096, 2048], P(('rep', 'shard')), may hold values from -6 to 6
Outputs:
- output: bfloat16 [4096, 2048], P(('rep', 'shard'))
- input_grad: bfloat16 [4096, 2048], P(('rep', 'shard'))
- first_gain_grad: float32 [2048], P('shard')
- first_shift_grad: float32 [2048], P('shard')
- project_weight_grad: float32 [2048, 6144], P('shard')
- project_bias_grad: float32 [6144], P('shard')
- mixing_weight_grad: float32 [2048, 2048], P('shard')
- mixing_bias_grad: float32 [2048], P('shard')
- second_gain_grad: float32 [2048], P('shard')
- second_shift_grad: float32 [2048], P('shard')
- widen_weight_grad: float32 [2048, 8192], P('shard')
- widen_bias_grad: float32 [8192], P('shard')
- narrow_weight_grad: float32 [8192, 2048], P('shard')
- narrow_bias_grad: float32 [2048], P('shard')
Inputs may be any that keep to these rules, and one draw needn't show every extreme that they name: `segment_ids`: documents never cross an aligned block of 128 tokens and begin only at positions within the block that are multiples of 8; in each block ids start at 0 and rise by one at each new document; some block holds 16 documents. `positions`: each token's position counts from 0 at the first token of its document; some block holds a single document.
All inputs are finite; a program needn't handle non-finite values.
Results may differ from a plain program's by a relative error of at most 0.015.
Values may be sent and summed in bfloat16 or wider, within the bound.
A program may use at most 640 MiB of HBM per device.

v0:
```python
import jax
import jax.numpy as jnp
from jax import lax
from jax.sharding import PartitionSpec as P

D = 2048
HEADS = 8
HEAD_DIM = 256
ROT = 64
FF = 8192


def layer_norm(values, gain, shift):
    center = values - jnp.mean(values, axis=-1, keepdims=True)
    spread = jnp.mean(center * center, axis=-1, keepdims=True)
    return center * lax.rsqrt(spread + 1e-05) * gain + shift


def angles(positions):
    freqs = 10000.0 ** (-(jnp.arange(ROT // 2, dtype=jnp.float32) * 2.0 / ROT))
    turned = positions.astype(jnp.float32)[..., None] * freqs
    return (jnp.cos(turned), jnp.sin(turned))


def rotary(values, cosine, sine):
    half = ROT // 2
    front = values[..., :half]
    back = values[..., half:ROT]
    return jnp.concatenate(
        [front * cosine - back * sine, back * cosine + front * sine, values[..., ROT:]], axis=-1
    )


def exact_gelu(values):
    return jax.nn.gelu(values, approximate=False)


def contract_rows(left, right):
    return lax.dot_general(
        left, right, (((0,), (0,)), ((), ())), preferred_element_type=jnp.float32
    )


def times_rows(left, piece):
    return lax.dot_general(
        left, piece, (((1,), (1,)), ((), ())), preferred_element_type=jnp.float32
    )


def weight_terms(left_one, left_two, left_mix, left_act, d_joint, d_widened, cotangent):

    def wide_term(start, count):
        return jnp.concatenate(
            [
                contract_rows(left_one, d_joint),
                contract_rows(left_two, d_widened),
                contract_rows(left_mix, cotangent),
            ],
            axis=1,
        )

    def down_term(start, count):
        return contract_rows(left_act, cotangent)

    return (wide_term, down_term)


def per_device(
    tokens,
    segment_ids,
    positions,
    first_gain,
    first_shift,
    project_weight,
    project_bias,
    mixing_weight,
    mixing_bias,
    second_gain,
    second_shift,
    widen_weight,
    widen_bias,
    narrow_weight,
    narrow_bias,
    cotangent,
):
    length = tokens.shape[0]
    shards = lax.axis_size("shard")
    gain_one, shift_one, gain_two, shift_two, joint_bias, mix_bias, wide_bias, narrow_full = (
        lax.all_gather(first_gain, "shard", axis=0, tiled=True),
        lax.all_gather(first_shift, "shard", axis=0, tiled=True),
        lax.all_gather(second_gain, "shard", axis=0, tiled=True),
        lax.all_gather(second_shift, "shard", axis=0, tiled=True),
        lax.all_gather(project_bias, "shard", axis=0, tiled=True),
        lax.all_gather(mixing_bias, "shard", axis=0, tiled=True),
        lax.all_gather(widen_bias, "shard", axis=0, tiled=True),
        lax.all_gather(narrow_bias, "shard", axis=0, tiled=True),
    )
    inputs = tokens.astype(jnp.float32)
    first_norm, first_pull = jax.vjp(layer_norm, inputs, gain_one, shift_one)
    second_norm, second_pull = jax.vjp(layer_norm, inputs, gain_two, shift_two)
    first = first_norm.astype(jnp.bfloat16)
    second = second_norm.astype(jnp.bfloat16)
    pieces = (
        lax.all_gather(project_weight, "shard", axis=0, tiled=True),
        lax.all_gather(widen_weight, "shard", axis=0, tiled=True),
    )
    part_one = jnp.dot(first, pieces[0], preferred_element_type=jnp.float32)
    part_two = jnp.dot(second, pieces[1], preferred_element_type=jnp.float32)
    joint = part_one + joint_bias
    widened = part_two + wide_bias
    shaped = joint.reshape(length, 3, HEADS, HEAD_DIM)
    cosine, sine = angles(positions)
    cosine = cosine[:, None, :]
    sine = sine[:, None, :]

    def place(query_in, key_in):
        return (rotary(query_in, cosine, sine) * HEAD_DIM ** (-0.5), rotary(key_in, cosine, sine))

    (query_turned, key_turned), rotate_pull = jax.vjp(place, shaped[:, 0], shaped[:, 1])
    query = query_turned.astype(jnp.bfloat16)
    keys = key_turned.astype(jnp.bfloat16)
    values = shaped[:, 2].astype(jnp.bfloat16)
    order = jnp.arange(length)
    allowed = ((segment_ids[:, None] == segment_ids[None, :]) & (order[:, None] >= order[None, :]))[
        None
    ]

    def masked_scores():
        raw = jnp.einsum("qhe,khe->hqk", query, keys, preferred_element_type=jnp.float32)
        return jnp.where(allowed, raw, -1e30)

    scores = masked_scores()
    highest = jnp.max(scores, axis=-1, keepdims=True)
    raised = jnp.exp(scores - highest)
    summed = jnp.sum(raised, axis=-1, keepdims=True)
    log_summed = highest + jnp.log(summed)
    weights = (raised / summed).astype(jnp.bfloat16)
    context = (
        jnp.einsum("hqk,khe->qhe", weights, values, preferred_element_type=jnp.float32)
        .reshape(length, D)
        .astype(jnp.bfloat16)
    )
    attention = (
        jnp.dot(
            context,
            lax.all_gather(mixing_weight, "shard", axis=0, tiled=True),
            preferred_element_type=jnp.float32,
        )
        + mix_bias
    )
    active_full, gelu_pull = jax.vjp(exact_gelu, widened)
    active = active_full.astype(jnp.bfloat16)
    mlp = (
        jnp.dot(
            active,
            lax.all_gather(narrow_weight, "shard", axis=0, tiled=True),
            preferred_element_type=jnp.float32,
        )
        + narrow_full
    )
    output = (inputs + attention + mlp).astype(jnp.bfloat16)

    def back_rows(piece):
        return times_rows(cotangent, piece)

    d_active = back_rows(lax.all_gather(narrow_weight, "shard", axis=0, tiled=True))
    d_widened = gelu_pull(d_active)[0].astype(jnp.bfloat16)
    d_context = back_rows(lax.all_gather(mixing_weight, "shard", axis=0, tiled=True))
    d_context = d_context.astype(jnp.bfloat16).reshape(length, HEADS, HEAD_DIM)
    again = jnp.exp(masked_scores() - log_summed)
    again_low = again.astype(jnp.bfloat16)
    d_weights = jnp.einsum("qhe,khe->hqk", d_context, values, preferred_element_type=jnp.float32)
    d_values = jnp.einsum("hqk,qhe->khe", again_low, d_context, preferred_element_type=jnp.float32)
    d_scores = (again * (d_weights - jnp.sum(d_weights * again, axis=-1, keepdims=True))).astype(
        jnp.bfloat16
    )
    d_query = jnp.einsum("hqk,khe->qhe", d_scores, keys, preferred_element_type=jnp.float32)
    d_keys = jnp.einsum("hqk,qhe->khe", d_scores, query, preferred_element_type=jnp.float32)
    d_query_in, d_key_in = rotate_pull((d_query, d_keys))
    d_joint = jnp.concatenate(
        [d_query_in.reshape(length, D), d_key_in.reshape(length, D), d_values.reshape(length, D)],
        axis=1,
    ).astype(jnp.bfloat16)
    pieces = lax.all_gather((project_weight, widen_weight), "shard", axis=0, tiled=True)
    stacked = jnp.concatenate(
        [times_rows(d_joint, pieces[0]), times_rows(d_widened, pieces[1])], axis=0
    )
    d_in_one, d_gain_one, d_shift_one = first_pull(stacked[:length])
    d_in_two, d_gain_two, d_shift_two = second_pull(stacked[length:])
    input_grad = (cotangent.astype(jnp.float32) + d_in_one + d_in_two).astype(jnp.bfloat16)
    sums = lax.psum(
        (
            d_gain_one,
            d_shift_one,
            d_gain_two,
            d_shift_two,
            jnp.sum(d_joint, axis=0, dtype=jnp.float32),
            jnp.sum(cotangent, axis=0, dtype=jnp.float32),
            jnp.sum(d_widened, axis=0, dtype=jnp.float32),
        ),
        ("rep", "shard"),
    )
    owner = lax.axis_index("shard")

    def own_part(vector):
        share = vector.shape[0] // shards
        return lax.dynamic_slice_in_dim(vector, owner * share, share)

    owned = [own_part(vector) for vector in sums]
    wide_term, down_term = weight_terms(
        first, second, context, active, d_joint, d_widened, cotangent
    )
    wide_part = lax.psum_scatter(
        wide_term(jnp.int32(0), lax.axis_size("shard") * (D // shards)).astype(jnp.bfloat16),
        "shard",
        scatter_dimension=0,
        tiled=True,
    ).astype(jnp.float32)
    down_part = lax.psum_scatter(
        down_term(jnp.int32(0), lax.axis_size("shard") * (FF // shards)).astype(jnp.bfloat16),
        "shard",
        scatter_dimension=0,
        tiled=True,
    ).astype(jnp.float32)
    wide_part, down_part = (
        lax.psum(wide_part.astype(jnp.bfloat16), "rep").astype(jnp.float32),
        lax.psum(down_part.astype(jnp.bfloat16), "rep").astype(jnp.float32),
    )
    return (
        output,
        input_grad,
        owned[0],
        owned[1],
        wide_part[:, : 3 * D],
        owned[4],
        wide_part[:, 3 * D + FF :],
        owned[5],
        owned[2],
        owned[3],
        wide_part[:, 3 * D : 3 * D + FF],
        owned[6],
        down_part,
        owned[5],
    )


def solution(mesh):
    in_specs = (
        P(("rep", "shard"), None),
        P(("rep", "shard")),
        P(("rep", "shard")),
        P("shard"),
        P("shard"),
        P("shard", None),
        P("shard"),
        P("shard", None),
        P("shard"),
        P("shard"),
        P("shard"),
        P("shard", None),
        P("shard"),
        P("shard", None),
        P("shard"),
        P(("rep", "shard"), None),
    )
    out_specs = (
        P(("rep", "shard"), None),
        P(("rep", "shard"), None),
        P("shard"),
        P("shard"),
        P("shard", None),
        P("shard"),
        P("shard", None),
        P("shard"),
        P("shard"),
        P("shard"),
        P("shard", None),
        P("shard"),
        P("shard", None),
        P("shard"),
    )
    return jax.shard_map(
        per_device, mesh=mesh, in_specs=in_specs, out_specs=out_specs, check_vma=False
    )
```

profile of v0, /device:TPU:0, one launch (start us, length us, event | category | flops | bytes accessed | tf_op | source)
XLA Modules:
  0.0 3883.6 jit_solution(1283411526838267227)
XLA Ops:
  7.2 0.7 all-gather.16.cloned.1.call-update
  8.0 0.7 all-gather.18.cloned.1.call-update
  8.7 0.7 all-gather.14.cloned.1.call-update
  10.1 63.1 %all-gather.4 = f32[8,1,256]{2,1,0:T(1,128)S(1)} all-gather(f32[1,1,256]{2,1,0:T(1,128)S(1)} %bitcast.99), channel_id=1, replica_groups=mesh['rep'=4,'shard'=8] {'shard'}, dimensions={0}, use_global_device_ids=true | all-gather | bytes 9216 | tf_op jit(solution)/shard_map/all_gather | solution.py:91
  73.2 24.2 all-gather.5
  97.4 45.8 %all_gather.49 = f32[8192]{0:T(1024)S(1)} all-gather(f32[1024]{0:T(1024)S(1)} %copy-done.14), channel_id=1, replica_groups=mesh['rep'=4,'shard'=8] {'shard'}, dimensions={0}, use_global_device_ids=true | all-gather | bytes 36864 | tf_op jit(solution)/shard_map/all_gather | solution.py:95
  143.6 507.2 %all-gather.16.cloned.1.call-done = bf16[2048,8192]{1,0:T(8,128)(2,1)} async-done(((bf16[256,8192]{1,0:T(8,128)(2,1)}), bf16[2048,8192]{1,0:T(8,128)(2,1)}) %all-gather.16.cloned.1.call-update) | async-done | bytes 33554448 | tf_op jit(solution)/shard_map/all_gather | solution.py:105
  650.9 18.3 convolution_add_fusion
  669.1 621.0 %all-gather.18.cloned.1.call-done = bf16[8192,2048]{1,0:T(8,128)(2,1)} async-done(((bf16[1024,2048]{1,0:T(8,128)(2,1)}), bf16[8192,2048]{1,0:T(8,128)(2,1)}) %all-gather.18.cloned.1.call-update) | async-done | bytes 33554448 | tf_op jit(solution)/shard_map/all_gather | solution.py:156
  1290.1 26.8 convert_reduce_fusion
  1316.9 4.0 multiply_convert_fusion
  1320.9 1.3 copy-done.1
  1322.2 13.8 convolution_convert_fusion.1
  1336.7 19.6 all-gather
  1356.3 16.5 all-gather.1
  1372.8 30.8 all-gather.2
  1404.0 13.8 all-gather.14.cloned.1.call-done
  1417.7 7.1 convolution_convert_fusion.4
  1424.8 2.1 copy.91
  1426.9 470.9 %all-gather.12.cloned.1.call-done = bf16[2048,6144]{1,0:T(8,128)(2,1)} async-done(((bf16[256,6144]{1,0:T(8,128)(2,1)}), bf16[2048,6144]{1,0:T(8,128)(2,1)}) %all-gather.12.cloned.1.call-update) | async-done | bytes 25165840 | tf_op jit(solution)/shard_map/all_gather | solution.py:104
  1897.8 10.3 convolution_add_fusion.1
  1908.2 1.0 copy.93
  1909.2 1.7 copy-done.3
  1910.9 1.2 copy.92
  1912.1 1.7 fusion.55
  1915.4 0.7 fusion.31
  1917.9 0.7 fusion.19
  1918.6 1.3 split.24
  1919.9 1.3 multiply_add_fusion.3
  1921.2 1.4 add_convert_fusion.1
  1922.6 2.1 copy.75
  1924.7 3.0 add_convert_fusion.2
  1927.7 2.0 copy.71
  1929.7 2.2 convolution_convert_fusion.5
  1931.9 1.4 convolution_convert_fusion.6
  1933.3 5.7 convolution_convert_fusion.3
  1939.0 13.6 convolution_convert_fusion.2
  1952.6 14.0 convolution_convert_fusion
  1966.6 44.7 %pad_maximum_fusion = bf16[2048,16384]{1,0:T(8,128)(2,1)} fusion(bf16[2048,2048]{1,0:T(8,128)(2,1)} %convolution_convert_fusion.3, bf16[2048,8192]{1,0:T(8,128)(2,1)} %convolution_convert_fusion, bf16[2048,6144]{1,0:T(8,128)(2,1)} %convolution_convert_fusion.2), kind=kLoop, calls=%fused_computation | loop fusion | flops 201326592 | bytes 134217728 | tf_op jit(solution)/shard_map/concatenate | solution.py:53
  2011.4 2.3 convert_reduce_fusion.1
  2013.7 17.3 fusion.57
  2031.1 15.2 fusion.53
  2046.3 2.7 fusion.27
  2049.0 3.5 convert_reduce_fusion.3
  2052.6 392.1 %reduce-scatter.5.cloned.1.call-done = bf16[1024,2048]{1,0:T(8,128)(2,1)} async-done(((bf16[8192,2048]{1,0:T(8,128)(2,1)}), bf16[1024,2048]{1,0:T(8,128)(2,1)}) %reduce-scatter.5.cloned.1.call-update) | async-done | bytes 4194320 | tf_op jit(solution)/shard_map/reduce_scatter | solution.py:219
  2444.6 1058.5 %reduce-scatter.3.cloned.1.call-done = bf16[256,16384]{1,0:T(8,128)(2,1)} async-done(((bf16[2048,16384]{1,0:T(8,128)(2,1)}), bf16[256,16384]{1,0:T(8,128)(2,1)}) %reduce-scatter.3.cloned.1.call-update) | async-done | bytes 8388624 | tf_op jit(solution)/shard_map/reduce_scatter | solution.py:213
  3503.2 0.6 copy-done.24
  3503.8 18.6 all-gather.3
  3522.4 16.3 all-gather.6
  3538.7 4.8 fusion.7
  3543.5 14.2 fusion.8
  3557.7 76.2 %all-reduce.11.cloned.1.call-done = (f32[2048]{0:T(1024)}, f32[2048]{0:T(1024)}, f32[6144]{0:T(1024)}, f32[2048]{0:T(1024)}, f32[2048]{0:T(1024)}, /*index=5*/f32[2048]{0:T(1024)}, f32[8192]{0:T(1024)}) async-done(((f32[2048]{0:T(1024)}, f32[2048]{0:T(1024)}, f32[6144]{0:T(1024)}, f32[2048]{0:T(1024)}, f32[2048]{0:T(1024)}, /*index=5*/f32[2048]{0:T(1024)}, f32[8192]{0:T(1024)}), (f32[2048]{0:T(1024)}, ...) | async-done | bytes 98320 | tf_op jit(solution)/shard_map/psum | solution.py:191
  3633.8 1.3 dynamic_slice.21
  3635.1 0.7 dynamic_slice.24
  3635.9 1.3 dynamic_slice.22
  3637.2 1.3 dynamic_slice.25
  3638.5 1.3 dynamic_slice.26
  3639.8 1.4 dynamic_slice.23
  3641.2 1.3 dynamic_slice.27
  3642.4 216.2 %all-reduce.13.cloned.1.call-done = (bf16[256,16384]{1,0:T(8,128)(2,1)}, bf16[1024,2048]{1,0:T(8,128)(2,1)}) async-done(((bf16[256,16384]{1,0:T(8,128)(2,1)}, bf16[1024,2048]{1,0:T(8,128)(2,1)}), (bf16[256,16384]{1,0:T(8,128)(2,1)}, bf16[1024,2048]{1,0:T(8,128)(2,1)})) %all-reduce.13.cloned.1.call-update) | async-done | bytes 12582928 | tf_op jit(solution)/shard_map/psum | solution.py:226
  3858.7 2.9 slice.60
  3861.6 5.5 slice.59
  3867.1 4.4 slice.61
  3871.5 4.4 convert_element_type.100
  (95 shorter events, 6.5 us)
Async XLA Ops:
  7.2 643.7 %all-gather.16.cloned.1.call-start = ((), (), s32[]{:S(2)}) async-start(), calls=%async_computation.4 | async-start | bytes 37748736 | tf_op jit(solution)/shard_map/all_gather | solution.py:105
  7.9 2.1 copy-start.20
  7.9 65.2 %copy-start.21 = (f32[256]{0:T(256)S(1)}, f32[256]{0:T(256)}, u32[]{:S(2)}) copy-start(f32[256]{0:T(256)} %param.26) | copy-start | bytes 3076
  7.9 89.5 %copy-start.14 = (f32[1024]{0:T(1024)S(1)}, f32[1024]{0:T(1024)}, u32[]{:S(2)}) copy-start(f32[1024]{0:T(1024)} %param.28) | copy-start | bytes 12292
  7.9 135.2 %copy-start = (bf16[128,2048]{1,0:T(8,128)(2,1)S(1)}, bf16[128,2048]{1,0:T(8,128)(2,1)}, u32[]{:S(2)}) copy-start(bf16[128,2048]{1,0:T(8,128)(2,1)} %param.16) | copy-start | bytes 1572868
  8.0 1282.2 %all-gather.18.cloned.1.call-start = ((), (), s32[]{:S(2)}) async-start(), calls=%async_computation.5 | async-start | bytes 37748736 | tf_op jit(solution)/shard_map/all_gather | solution.py:156
  8.7 1409.0 %all-gather.14.cloned.1.call-start = ((), (), s32[]{:S(2)}) async-start(), calls=%async_computation.3 | async-start | bytes 9437184 | tf_op jit(solution)/shard_map/all_gather | solution.py:146
  9.4 1888.4 %all-gather.12.cloned.1.call-start = ((), (), s32[]{:S(2)}) async-start(), calls=%async_computation.2 | async-start | bytes 28311552 | tf_op jit(solution)/shard_map/all_gather | solution.py:104
  10.0 2434.6 %reduce-scatter.5.cloned.1.call-start = ((), (), s32[]{:S(2)}) async-start(), calls=%async_computation.7 | async-start | bytes 37748736 | tf_op jit(solution)/shard_map/reduce_scatter | solution.py:219
  143.6 525.5 %copy-start.18 = (f32[128]{0:T(128)}, f32[128]{0:T(128)S(1)}, u32[]{:S(2)}) copy-start(f32[128]{0:T(128)S(1)} %fusion.28) | copy-start | bytes 1540
  650.9 639.2 %copy-start.5 = (bf16[128,2048]{1,0:T(8,128)(2,1)S(1)}, bf16[128,2048]{1,0:T(8,128)(2,1)}, u32[]{:S(2)}) copy-start(bf16[128,2048]{1,0:T(8,128)(2,1)} %param.31) | copy-start | bytes 1572868
  1320.9 1.3 copy-start.1
  1336.0 0.7 copy-start.26
  1336.0 0.7 copy-start.15
  1336.0 0.7 copy-start.22
  1336.0 20.3 copy-start.23
  1336.0 67.6 %copy-start.17 = (s32[128]{0:T(128)S(1)}, s32[128]{0:T(128)}, u32[]{:S(2)}) copy-start(s32[128]{0:T(128)} %param.17) | copy-start | bytes 1540
  1336.0 2167.1 %reduce-scatter.3.cloned.1.call-start = ((), (), s32[]{:S(2)}) async-start(), calls=%async_computation.6 | async-start | bytes 75497472 | tf_op jit(solution)/shard_map/reduce_scatter | solution.py:213
  1909.2 1.7 copy-start.3
  1914.9 1.8 copy-start.11
  1915.0 1.8 copy-start.13
  1929.7 3.6 copy-start.6
  1933.3 5.8 copy-start.8
  1933.3 5.7 copy-start.10
  2011.4 1622.5 %all-reduce.11.cloned.1.call-start = ((), (), s32[]{:S(2)}) async-start(), calls=%async_computation.8 | async-start | bytes 196608 | tf_op jit(solution)/shard_map/psum | solution.py:191
  2031.0 15.2 copy-start.19
  2031.0 15.3 copy-start.4
  2031.0 18.0 copy-start.7
  2052.5 1806.2 %all-reduce.13.cloned.1.call-start = ((), (), s32[]{:S(2)}) async-start(), calls=%async_computation.9 | async-start | bytes 25165824 | tf_op jit(solution)/shard_map/psum | solution.py:226
  3503.2 0.7 copy-start.24
  3503.2 19.2 copy-start.25
  3503.2 35.5 copy-start.9
  3538.7 4.8 copy-start.2
  3635.9 240.1 %copy-start.16 = (f32[256]{0:T(256)}, f32[256]{0:T(256)S(1)}, u32[]{:S(2)}) copy-start(f32[256]{0:T(256)S(1)} %dynamic_slice.24) | copy-start | bytes 3076
  3858.7 8.4 slice-start
  3861.6 5.5 slice-start.1
  3867.1 4.4 copy-start.12
Sparse Core Ops, SparseCore 0:
  9.5 641.2 all-gather.15
  652.4 637.6 all-gather.17
  1292.2 125.4 all-gather.13
  1419.1 478.6 all-gather.11
  1901.4 543.1 reduce-scatter.4
  2448.3 1054.8 reduce-scatter.2
  3510.7 123.0 all-reduce.10
  3636.7 221.9 all-reduce.12
where the time goes:
time: 3890 us; the launch traced here: 3880 us
  waiting for transfers between devices  3360 us (86%)
  blocking collectives  235 us (6%)
  matrix products  166 us (4%)
  other arithmetic  69.5 us (2%)
  local copies, waits for them, and re-layouts  39.2 us (1%)
    reduce_scatter x1, waiting for transfers between devices, per_device(): lax.psum_scatter(wide_term(jnp.int32(0), lax.axis_size('shard') * (D // s...  1060 us
    all_gather x1, waiting for transfers between devices, per_device(): lax.all_gather(narrow_weight, 'shard', axis=0, tiled=True)  621 us
    all_gather x1, waiting for transfers between devices, per_device(): lax.all_gather(widen_weight, 'shard', axis=0, tiled=True)  507 us
    all_gather x1, waiting for transfers between devices, per_device(): lax.all_gather(project_weight, 'shard', axis=0, tiled=True)  471 us
    reduce_scatter x1, waiting for transfers between devices, per_device(): lax.psum_scatter(down_term(jnp.int32(0), lax.axis_size('shard') * (FF //...  392 us
    psum x1, waiting for transfers between devices, per_device(): lax.psum(wide_part.astype(jnp.bfloat16), 'rep').astype(jnp.float32)  216 us
  transfers between devices with their start and end apart: 8, of which 8 were waited for; matrix products, arithmetic and copies ran while one was open for 7% of the time, Pallas kernels for 0%

commit v1 on v0

--- a/solution.py
+++ b/solution.py
@@ -8,6 +8,19 @@
 HEAD_DIM = 256
 ROT = 64
 FF = 8192
+
+
+def ring_gather(array, axis, dim):
+    ways = lax.axis_size(axis)
+    up = [(d, (d + 1) % ways) for d in range(ways)]
+    down = [(d, (d - 1) % ways) for d in range(ways)]
+    earlier, later = ([array], [array])
+    for _ in range(ways // 2):
+        earlier.append(lax.ppermute(earlier[-1], axis, up))
+    for _ in range((ways - 1) // 2):
+        later.append(lax.ppermute(later[-1], axis, down))
+    line = jnp.concatenate([*earlier[::-1], *later[1:]], axis=dim)
+    return jnp.roll(line, (lax.axis_index(axis) - ways // 2) * array.shape[dim], axis=dim)
 
 
 def layer_norm(values, gain, shift):
@@ -102,7 +115,7 @@
     second = second_norm.astype(jnp.bfloat16)
     pieces = (
         lax.all_gather(project_weight, "shard", axis=0, tiled=True),
-        lax.all_gather(widen_weight, "shard", axis=0, tiled=True),
+        ring_gather(widen_weight, "shard", 0),
     )
     part_one = jnp.dot(first, pieces[0], preferred_element_type=jnp.float32)
     part_two = jnp.dot(second, pieces[1], preferred_element_type=jnp.float32)

time: 3890 us -> 4530 us (1.16)
  waiting for transfers between devices: 3360 us -> 3760 us
  blocking collectives: 235 us -> 396 us
  local copies, waits for them, and re-layouts: 39.2 us -> 100 us
    ppermute x0 -> x7, waiting for transfers between devices: none -> 957 us  [the longest x4 898 us: ring_gather(): earlier.append(lax.ppermute(earlier[-1], axis, up))]
    all_gather x1, waiting for transfers between devices: 621 us -> 0.01 us  [per_device(): lax.all_gather(narrow_weight, 'shard', axis=0, tiled=True)]
    reduce_scatter x1, waiting for transfers between devices: 392 us -> 507 us  [per_device(): lax.psum_scatter(down_term(jnp.int32(0), lax.axis_size('shard') * (FF //...]
    all_gather x1, blocking collectives: 24.2 us -> 131 us  [per_device(): lax.all_gather(second_shift, 'shard', axis=0, tiled=True)]
    unnamed x62 -> x91, local copies, waits for them, and re-layouts: 7.08 us -> 66.7 us
    all_gather x1, waiting for transfers between devices: 471 us -> 418 us  [per_device(): lax.all_gather(project_weight, 'shard', axis=0, tiled=True)]
  transfers between devices with their start and end apart: 8 -> 15, of which waited for: 8 -> 10; matrix products, arithmetic and copies ran while one was open for 7% -> 7% of each run, Pallas kernels for 0% -> 0%
where the time goes in v1:
time: 4530 us; the launch traced here: 4520 us
  waiting for transfers between devices  3760 us (83%)
  blocking collectives  396 us (9%)
  matrix products  164 us (4%)
  local copies, waits for them, and re-layouts  100 us (2%)
  other arithmetic  71.3 us (2%)
    reduce_scatter x1, waiting for transfers between devices, per_device(): lax.psum_scatter(wide_term(jnp.int32(0), lax.axis_size('shard') * (D // s...  1060 us
    ppermute x4, waiting for transfers between devices, ring_gather(): earlier.append(lax.ppermute(earlier[-1], axis, up))  898 us
    all_gather x1, waiting for transfers between devices, per_device(): lax.all_gather((project_weight, widen_weight), 'shard', axis=0, tiled=True)  522 us
    reduce_scatter x1, waiting for transfers between devices, per_device(): lax.psum_scatter(down_term(jnp.int32(0), lax.axis_size('shard') * (FF //...  507 us
    all_gather x1, waiting for transfers between devices, per_device(): lax.all_gather(project_weight, 'shard', axis=0, tiled=True)  418 us
    psum x1, waiting for transfers between devices, per_device(): lax.psum(wide_part.astype(jnp.bfloat16), 'rep').astype(jnp.float32)  216 us
    all_gather x1, blocking collectives, per_device(): lax.all_gather(second_shift, 'shard', axis=0, tiled=True)  131 us
  transfers between devices with their start and end apart: 15, of which 10 were waited for; matrix products, arithmetic and copies ran while one was open for 7% of the time, Pallas kernels for 0%

profile of v1, /device:TPU:0, one launch (start us, length us, event | category | flops | bytes accessed | tf_op | source)
XLA Modules:
  0.0 4521.4 jit_solution(14241532369449106482)
XLA Ops:
  10.1 3.0 collective-permute-start
  13.1 191.3 %collective-permute-done = bf16[256,8192]{1,0:T(8,128)(2,1)S(1)} collective-permute-done((bf16[256,8192]{1,0:T(8,128)(2,1)}, bf16[256,8192]{1,0:T(8,128)(2,1)S(1)}, u32[]{:S(2)}, u32[]{:S(2)}) %collective-permute-start) | collective-permute-done | bytes 4194336 | tf_op jit(solution)/shard_map/ppermute | solution.py:19
  206.4 2.4 collective-permute-start.1
  208.7 3.0 collective-permute-start.4
  211.8 394.6 %collective-permute-done.1 = bf16[256,8192]{1,0:T(8,128)(2,1)S(1)} collective-permute-done((bf16[256,8192]{1,0:T(8,128)(2,1)S(1)}, bf16[256,8192]{1,0:T(8,128)(2,1)S(1)}, u32[]{:S(2)}, u32[]{:S(2)}) %collective-permute-start.1) | collective-permute-done | bytes 4194336 | tf_op jit(solution)/shard_map/ppermute | solution.py:19
  608.4 2.5 collective-permute-start.2
  610.8 2.2 collective-permute-start.5
  613.1 312.0 %collective-permute-done.2 = bf16[256,8192]{1,0:T(8,128)(2,1)} collective-permute-done((bf16[256,8192]{1,0:T(8,128)(2,1)S(1)}, bf16[256,8192]{1,0:T(8,128)(2,1)}, u32[]{:S(2)}, u32[]{:S(2)}) %collective-permute-start.2) | collective-permute-done | bytes 4194336 | tf_op jit(solution)/shard_map/ppermute | solution.py:19
  925.1 3.0 collective-permute-start.3
  928.1 131.0 %all-gather.5 = f32[8,1,256]{2,1,0:T(1,128)S(1)} all-gather(f32[1,1,256]{2,1,0:T(1,128)S(1)} %bitcast.96), channel_id=1, replica_groups=mesh['rep'=4,'shard'=8] {'shard'}, dimensions={0}, use_global_device_ids=true | all-gather | bytes 9216 | tf_op jit(solution)/shard_map/all_gather | solution.py:105
  1059.1 85.9 %all-gather.4 = f32[8,1,256]{2,1,0:T(1,128)S(1)} all-gather(f32[1,1,256]{2,1,0:T(1,128)S(1)} %bitcast.97), channel_id=1, replica_groups=mesh['rep'=4,'shard'=8] {'shard'}, dimensions={0}, use_global_device_ids=true | all-gather | bytes 9216 | tf_op jit(solution)/shard_map/all_gather | solution.py:104
  1145.0 47.6 %all_gather.47 = f32[8192]{0:T(1024)S(1)} all-gather(f32[1024]{0:T(1024)S(1)} %copy-done.23), channel_id=1, replica_groups=mesh['rep'=4,'shard'=8] {'shard'}, dimensions={0}, use_global_device_ids=true | all-gather | bytes 36864 | tf_op jit(solution)/shard_map/all_gather | solution.py:108
  1193.1 4.6 constant_dynamic-update-slice_fusion.15
  1197.7 4.8 constant_dynamic-update-slice_fusion.14
  1202.5 2.4 constant_dynamic-update-slice_fusion.13
  1206.2 2.4 constant_dynamic-update-slice_fusion.12
  1209.9 2.2 constant_dynamic-update-slice_fusion.11
  1212.1 4.6 constant_dynamic-update-slice_fusion.10
  1216.7 4.6 constant_dynamic-update-slice_fusion.9
  1221.3 58.8 %collective-permute-done.6 = bf16[256,8192]{1,0:T(8,128)(2,1)S(1)} collective-permute-done((bf16[256,8192]{1,0:T(8,128)(2,1)}, bf16[256,8192]{1,0:T(8,128)(2,1)S(1)}, u32[]{:S(2)}, u32[]{:S(2)}) %collective-permute-start.6) | collective-permute-done | bytes 4194336 | tf_op jit(solution)/shard_map/ppermute | solution.py:21
  1280.1 2.2 constant_dynamic-update-slice_fusion.8
  1282.4 4.7 constant_dynamic-update-slice_fusion.7
  1287.1 4.6 constant_dynamic-update-slice_fusion.6
  1291.7 2.2 constant_dynamic-update-slice_fusion.5
  1293.9 2.2 constant_dynamic-update-slice_fusion.4
  1296.1 2.3 constant_dynamic-update-slice_fusion.3
  1298.5 5.1 constant_dynamic-update-slice_fusion.2
  1303.6 4.6 constant_dynamic-update-slice_fusion.1
  1308.1 2.3 constant_dynamic-update-slice_fusion
  1310.4 15.4 fusion.2
  1325.8 26.7 convert_reduce_fusion
  1352.4 3.9 multiply_convert_fusion
  1357.7 13.8 convolution_convert_fusion.1
  1372.2 19.0 all-gather.1
  1391.2 16.4 all-gather
  1407.6 61.5 %all-gather.2 = f32[8,1,768]{2,1,0:T(1,128)S(1)} all-gather(f32[1,1,768]{2,1,0:T(1,128)S(1)} %reshape.214), channel_id=1, replica_groups=mesh['rep'=4,'shard'=8] {'shard'}, dimensions={0}, use_global_device_ids=true | all-gather | bytes 27648 | tf_op jit(solution)/shard_map/all_gather | solution.py:106
  1469.5 7.2 convolution_convert_fusion.4
  1476.7 2.1 copy.91
  1478.8 418.3 %all-gather.12.cloned.1.call-done = bf16[2048,6144]{1,0:T(8,128)(2,1)} async-done(((bf16[256,6144]{1,0:T(8,128)(2,1)}), bf16[2048,6144]{1,0:T(8,128)(2,1)}) %all-gather.12.cloned.1.call-update) | async-done | bytes 25165840 | tf_op jit(solution)/shard_map/all_gather | solution.py:117
  1897.1 10.3 convolution_add_fusion
  1925.0 3.0 add_convert_fusion.2
  1928.0 2.1 copy.71
  1930.0 2.2 convolution_convert_fusion.5
  1933.6 5.7 convolution_convert_fusion.3
  1939.4 13.4 convolution_convert_fusion.2
  1952.8 14.1 convolution_convert_fusion
  1966.9 45.0 pad_maximum_fusion
  2012.0 2.3 convert_reduce_fusion.1
  2014.3 521.8 %all-gather.18.cloned.1.call-done = bf16[2048,8192]{1,0:T(8,128)(2,1)} async-done(((bf16[256,8192]{1,0:T(8,128)(2,1)}), bf16[2048,8192]{1,0:T(8,128)(2,1)}) %all-gather.18.cloned.1.call-update) | async-done | bytes 33554448 | tf_op jit(solution)/shard_map/all_gather | solution.py:197
  2536.2 17.7 fusion.63
  2553.9 15.2 fusion.59
  2569.2 2.7 fusion.32
  2571.9 3.5 convert_reduce_fusion.3
  2575.4 507.3 %reduce-scatter.5.cloned.1.call-done = bf16[1024,2048]{1,0:T(8,128)(2,1)} async-done(((bf16[8192,2048]{1,0:T(8,128)(2,1)}), bf16[1024,2048]{1,0:T(8,128)(2,1)}) %reduce-scatter.5.cloned.1.call-update) | async-done | bytes 4194320 | tf_op jit(solution)/shard_map/reduce_scatter | solution.py:232
  3082.7 1059.6 %reduce-scatter.3.cloned.1.call-done = bf16[256,16384]{1,0:T(8,128)(2,1)} async-done(((bf16[2048,16384]{1,0:T(8,128)(2,1)}), bf16[256,16384]{1,0:T(8,128)(2,1)}) %reduce-scatter.3.cloned.1.call-update) | async-done | bytes 8388624 | tf_op jit(solution)/shard_map/reduce_scatter | solution.py:226
  4142.9 18.6 all-gather.3
  4161.5 16.3 all-gather.6
  4177.8 4.8 fusion.12
  4182.6 14.2 fusion.13
  4196.8 76.1 %all-reduce.11.cloned.1.call-done = (f32[2048]{0:T(1024)}, f32[2048]{0:T(1024)}, f32[6144]{0:T(1024)}, f32[2048]{0:T(1024)}, f32[2048]{0:T(1024)}, /*index=5*/f32[2048]{0:T(1024)}, f32[8192]{0:T(1024)}) async-done(((f32[2048]{0:T(1024)}, f32[2048]{0:T(1024)}, f32[6144]{0:T(1024)}, f32[2048]{0:T(1024)}, f32[2048]{0:T(1024)}, /*index=5*/f32[2048]{0:T(1024)}, f32[8192]{0:T(1024)}), (f32[2048]{0:T(1024)}, ...) | async-done | bytes 98320 | tf_op jit(solution)/shard_map/psum | solution.py:204
  4281.5 216.3 %all-reduce.13.cloned.1.call-done = (bf16[256,16384]{1,0:T(8,128)(2,1)}, bf16[1024,2048]{1,0:T(8,128)(2,1)}) async-done(((bf16[256,16384]{1,0:T(8,128)(2,1)}, bf16[1024,2048]{1,0:T(8,128)(2,1)}), (bf16[256,16384]{1,0:T(8,128)(2,1)}, bf16[1024,2048]{1,0:T(8,128)(2,1)})) %all-reduce.13.cloned.1.call-update) | async-done | bytes 12582928 | tf_op jit(solution)/shard_map/psum | solution.py:239
  4497.8 5.5 slice.59
  4505.0 4.4 slice.61
  4509.4 4.4 convert_element_type.100
  (138 shorter events, 42.8 us)
Async XLA Ops:
  7.2 1318.6 %all-gather.16.cloned.1.call-start = ((), (), s32[]{:S(2)}) async-start(), calls=%async_computation.4 | async-start | bytes 37748736 | tf_op jit(solution)/shard_map/all_gather | solution.py:169
  7.9 920.2 %copy-start.29 = (f32[256]{0:T(256)S(1)}, f32[256]{0:T(256)}, u32[]{:S(2)}) copy-start(f32[256]{0:T(256)} %param.26) | copy-start | bytes 3076
  7.9 1051.2 %copy-start.30 = (f32[256]{0:T(256)S(1)}, f32[256]{0:T(256)}, u32[]{:S(2)}) copy-start(f32[256]{0:T(256)} %param.25) | copy-start | bytes 3076
  7.9 1137.1 %copy-start.23 = (f32[1024]{0:T(1024)S(1)}, f32[1024]{0:T(1024)}, u32[]{:S(2)}) copy-start(f32[1024]{0:T(1024)} %param.28) | copy-start | bytes 12292
  7.9 1184.6 %copy-start = (bf16[128,2048]{1,0:T(8,128)(2,1)S(1)}, bf16[128,2048]{1,0:T(8,128)(2,1)}, u32[]{:S(2)}) copy-start(bf16[128,2048]{1,0:T(8,128)(2,1)} %param.16) | copy-start | bytes 1572868
  8.0 1461.6 %all-gather.14.cloned.1.call-start = ((), (), s32[]{:S(2)}) async-start(), calls=%async_computation.3 | async-start | bytes 9437184 | tf_op jit(solution)/shard_map/all_gather | solution.py:159
  8.7 1888.4 %all-gather.12.cloned.1.call-start = ((), (), s32[]{:S(2)}) async-start(), calls=%async_computation.2 | async-start | bytes 28311552 | tf_op jit(solution)/shard_map/all_gather | solution.py:117
  9.4 2526.7 %all-gather.18.cloned.1.call-start = ((), (), s32[]{:S(2)}) async-start(), calls=%async_computation.5 | async-start | bytes 37748736 | tf_op jit(solution)/shard_map/all_gather | solution.py:197
  10.0 3072.7 %reduce-scatter.5.cloned.1.call-start = ((), (), s32[]{:S(2)}) async-start(), calls=%async_computation.7 | async-start | bytes 37748736 | tf_op jit(solution)/shard_map/reduce_scatter | solution.py:232
  10.1 194.3 %collective-permute-start = (bf16[256,8192]{1,0:T(8,128)(2,1)}, bf16[256,8192]{1,0:T(8,128)(2,1)S(1)}, u32[]{:S(2)}, u32[]{:S(2)}) collective-permute-start(bf16[256,8192]{1,0:T(8,128)(2,1)} %param.27), channel_id=1, source_target_pairs={{0,1},{1,2},{2,3},{3,4},{4,5},{5,6},{6,7},{7,0},{8,9},{9,10},{10,1... | collective-permute-start | bytes 12582920 | tf_op jit(solution)/shard_map/ppermute | solution.py:19
  204.3 2.0 copy-start.5
  206.4 400.0 %collective-permute-start.1 = (bf16[256,8192]{1,0:T(8,128)(2,1)S(1)}, bf16[256,8192]{1,0:T(8,128)(2,1)S(1)}, u32[]{:S(2)}, u32[]{:S(2)}) collective-permute-start(bf16[256,8192]{1,0:T(8,128)(2,1)S(1)} %collective-permute-done), channel_id=1, source_target_pairs={{0,1},{1,2},{2,3},{3,4},{4,5},{5,6},{6,7},{7,0},{8,9},{9,10},{10,1... | collective-permute-start | bytes 12582920 | tf_op jit(solution)/shard_map/ppermute | solution.py:19
  208.7 402.1 %collective-permute-start.4 = (bf16[256,8192]{1,0:T(8,128)(2,1)}, bf16[256,8192]{1,0:T(8,128)(2,1)}, u32[]{:S(2)}, u32[]{:S(2)}) collective-permute-start(bf16[256,8192]{1,0:T(8,128)(2,1)} %param.27), channel_id=1, source_target_pairs={{0,7},{1,0},{2,1},{3,2},{4,3},{5,4},{6,5},{7,6},{8,15},{9,8},{10,9... | collective-permute-start | bytes 12582920 | tf_op jit(solution)/shard_map/ppermute | solution.py:21
  606.3 2.0 copy-start.7
  608.4 316.7 %collective-permute-start.2 = (bf16[256,8192]{1,0:T(8,128)(2,1)S(1)}, bf16[256,8192]{1,0:T(8,128)(2,1)}, u32[]{:S(2)}, u32[]{:S(2)}) collective-permute-start(bf16[256,8192]{1,0:T(8,128)(2,1)S(1)} %collective-permute-done.1), channel_id=1, source_target_pairs={{0,1},{1,2},{2,3},{3,4},{4,5},{5,6},{6,7},{7,0},{8,9},{9,10},{10,1... | collective-permute-start | bytes 12582920 | tf_op jit(solution)/shard_map/ppermute | solution.py:19
  610.8 582.2 %collective-permute-start.5 = (bf16[256,8192]{1,0:T(8,128)(2,1)}, bf16[256,8192]{1,0:T(8,128)(2,1)}, u32[]{:S(2)}, u32[]{:S(2)}) collective-permute-start(bf16[256,8192]{1,0:T(8,128)(2,1)} %collective-permute-done.4), channel_id=1, source_target_pairs={{0,7},{1,0},{2,1},{3,2},{4,3},{5,4},{6,5},{7,6},{8,15},{9,8},{10,9... | collective-permute-start | bytes 12582920 | tf_op jit(solution)/shard_map/ppermute | solution.py:21
  925.1 268.1 %collective-permute-start.3 = (bf16[256,8192]{1,0:T(8,128)(2,1)}, bf16[256,8192]{1,0:T(8,128)(2,1)}, u32[]{:S(2)}, u32[]{:S(2)}) collective-permute-start(bf16[256,8192]{1,0:T(8,128)(2,1)} %collective-permute-done.2), channel_id=1, source_target_pairs={{0,1},{1,2},{2,3},{3,4},{4,5},{5,6},{6,7},{7,0},{8,9},{9,10},{10,1... | collective-permute-start | bytes 12582920 | tf_op jit(solution)/shard_map/ppermute | solution.py:19
  1193.0 4.7 copy-start.27
  1193.1 87.1 %collective-permute-start.6 = (bf16[256,8192]{1,0:T(8,128)(2,1)}, bf16[256,8192]{1,0:T(8,128)(2,1)S(1)}, u32[]{:S(2)}, u32[]{:S(2)}) collective-permute-start(bf16[256,8192]{1,0:T(8,128)(2,1)} %collective-permute-done.5), channel_id=1, source_target_pairs={{0,7},{1,0},{2,1},{3,2},{4,3},{5,4},{6,5},{7,6},{8,15},{9,8},{10,9... | collective-permute-start | bytes 12582920 | tf_op jit(solution)/shard_map/ppermute | solution.py:21
  1197.7 4.8 copy-start.8
  1202.5 3.7 copy-start.6
  1206.2 3.7 copy-start.1
  1310.4 15.4 copy-start.11
  1356.4 1.3 copy-start.3
  1371.5 0.7 copy-start.24
  1371.5 0.7 copy-start.35
  1371.5 0.7 copy-start.31
  1371.5 19.7 copy-start.32
  1371.5 97.6 %copy-start.26 = (s32[128]{0:T(128)S(1)}, s32[128]{0:T(128)}, u32[]{:S(2)}) copy-start(s32[128]{0:T(128)} %param.17) | copy-start | bytes 1540
  1371.5 2770.7 %reduce-scatter.3.cloned.1.call-start = ((), (), s32[]{:S(2)}) async-start(), calls=%async_computation.6 | async-start | bytes 75497472 | tf_op jit(solution)/shard_map/reduce_scatter | solution.py:226
  1909.3 1.0 copy-start.10
  1909.3 2.3 copy-start.14
  1913.8 2.0 copy-start.20
  1913.8 2.7 copy-start.22
  1913.8 3.4 copy-start.18
  1913.8 3.4 copy-start.21
  1930.0 3.6 copy-start.12
  1933.6 5.8 copy-start.15
  1933.6 5.7 copy-start.17
  2012.0 2260.9 %all-reduce.11.cloned.1.call-start = ((), (), s32[]{:S(2)}) async-start(), calls=%async_computation.8 | async-start | bytes 196608 | tf_op jit(solution)/shard_map/psum | solution.py:204
  2553.9 15.2 copy-start.28
  2553.9 15.3 copy-start.9
  2553.9 17.9 copy-start.13
  2575.4 1922.4 %all-reduce.13.cloned.1.call-start = ((), (), s32[]{:S(2)}) async-start(), calls=%async_computation.9 | async-start | bytes 25165824 | tf_op jit(solution)/shard_map/psum | solution.py:239
  4142.3 0.7 copy-start.33
  4142.3 19.3 copy-start.34
  4142.3 35.5 copy-start.16
  4177.8 4.8 copy-start.4
  4276.3 237.5 %copy-start.25 = (f32[256]{0:T(256)}, f32[256]{0:T(256)S(1)}, u32[]{:S(2)}) copy-start(f32[256]{0:T(256)S(1)} %dynamic_slice.29) | copy-start | bytes 3076
  4497.8 5.7 copy-start.2
  4505.0 4.4 copy-start.19
Sparse Core Ops, SparseCore 0:
  9.5 1278.0 all-gather.15
  1289.8 126.9 all-gather.13
  1418.3 478.7 all-gather.11
  1898.5 637.6 all-gather.17
  2539.8 542.8 reduce-scatter.4
  3086.3 1055.8 reduce-scatter.2
  4149.8 123.0 all-reduce.10
  4275.7 221.9 all-reduce.12
